TPU v7x, 128 devices: a whole 4x4x4 slice. The times are simulated.
128 devices in a mesh: sx: 8 (over x, z_hi), sy: 16 (over z_lo, y, core).
Axes of the slice: x: 4, y: 4, z: 4 (z_hi: 2, z_lo: 2; z = z_hi * 2 + z_lo), core: 2. Of those that a mesh axis runs over, the one named last changes fastest.
Arguments:
- interior_rhs: bfloat16 [8, 16, 2048, 1024], P('sx', 'sy'), may hold values from -6 to 6
- interface_coupling: bfloat16 [8, 16, 1024, 2048], P('sx', 'sy'), may hold values from -0.125 to 0.125
- interface_local: float32 [8, 16, 1024, 1024], P('sx', 'sy'), may hold values from -6 to 6
- off_blocks: bfloat16 [8, 16, 16, 4, 128, 128], P('sx', 'sy'), may hold values from -0.125 to 0.125
- diag_inverse: bfloat16 [8, 16, 16, 128, 128], P('sx', 'sy')
- block_pattern: int32 [8, 16, 16, 4], P('sx', 'sy'), may hold values from 0 to 15
- face_order: int32 [8, 16, 2, 512], P('sx', 'sy'), may hold values from 0 to 511, each once within a row
- krylov_map: int32 [8, 16, 1024], P('sx', 'sy'), may hold values from 0 to 1023, each once within a row
Outputs:
- krylov_rows: float32 [8, 16, 1024, 1024], P('sx', 'sy')
Inputs may be any that keep to these rules, and one draw needn't show every extreme that they name: Each face_order[i, j, f] is a permutation of 0 to 511. Each krylov_map[i, j] is a permutation of 0 to 1023.
All inputs are finite; a program needn't handle non-finite values.
Results may differ from a plain program's by a relative error of at most 0.0037.
Values sent between devices are 32-bit elements; how exact they have to be, the bound alone decides.
No kernel may reach another device: no remote copies, remote signals or barrier semaphores. Data moves between devices by JAX's collectives and lax.ppermute only.
A program may use at most 128 MiB of HBM per device.

v0:
```python
import jax
import jax.numpy as jnp
from jax import lax
from jax.sharding import PartitionSpec as P

BS = 128
FACE = 512
NB = 16
NNZ = 4
SWEEPS = 3
ROWS = 1024
NI = 2048


exact = lax.Precision.HIGHEST


def swapped(block, axis, bit):
    count = lax.axis_size(axis)
    route = []
    for low in range(count):
        high = low | 1 << bit
        if high != low and high < count:
            route += [(low, high), (high, low)]
    return lax.ppermute(block, axis, route)


def eliminate(rhs_cols, offs, dinv, pattern):
    width = rhs_cols.shape[1]
    blocks = rhs_cols.reshape(NB, BS, width)
    picker = (pattern[:, :, None] == jnp.arange(NB, dtype=jnp.int32)[None, None, :]).astype(
        jnp.bfloat16
    )
    picker = picker.reshape(NB * NNZ, NB)
    z_now = jnp.einsum("bij,bjc->bic", dinv, blocks, preferred_element_type=jnp.float32).astype(
        jnp.bfloat16
    )
    for sweep in range(SWEEPS):
        nearby = jnp.dot(picker, z_now.reshape(NB, BS * width), preferred_element_type=jnp.float32)
        nearby = nearby.astype(jnp.bfloat16).reshape(NB, NNZ, BS, width)
        acc = jnp.einsum("bkij,bkjc->bic", offs, nearby, preferred_element_type=jnp.float32)
        resid = (blocks.astype(jnp.float32) - acc).astype(jnp.bfloat16)
        z_now = jnp.einsum("bij,bjc->bic", dinv, resid, preferred_element_type=jnp.float32).astype(
            jnp.bfloat16
        )
    return z_now.reshape(NI, width)


def perm_matrix(order, count):
    return (order[:, None] == jnp.arange(count, dtype=jnp.int32)[None, :]).astype(jnp.float32)


def to_shared(block, order):
    picker = perm_matrix(order, FACE)
    left = jnp.dot(picker, block, precision=exact, preferred_element_type=jnp.float32)
    return jnp.dot(left, picker.T, precision=exact, preferred_element_type=jnp.float32)


def to_local(block, order):
    picker = perm_matrix(order, FACE)
    left = jnp.dot(picker.T, block, precision=exact, preferred_element_type=jnp.float32)
    return jnp.dot(left, picker, precision=exact, preferred_element_type=jnp.float32)


def assemble_a(block, order):
    partner = swapped(to_shared(block, order), "sx", 0)
    return block + to_local(partner, order)


def assemble_b(block, order):
    partner = swapped(to_shared(block, order), "sy", 0)
    return block + to_local(partner, order)


def place_rows(tile, target):
    placer = perm_matrix(target, ROWS).T
    return jnp.dot(placer, tile, precision=exact, preferred_element_type=jnp.float32)


def local(
    interior_rhs,
    interface_coupling,
    interface_local,
    off_blocks,
    diag_inverse,
    block_pattern,
    face_order,
    krylov_map,
):
    rhs = interior_rhs[0, 0]
    coupling = interface_coupling[0, 0]
    own = interface_local[0, 0]
    offs = off_blocks[0, 0]
    dinv = diag_inverse[0, 0]
    pattern = block_pattern[0, 0]
    orders = face_order[0, 0]
    target = krylov_map[0, 0]
    z_all = eliminate(rhs, offs, dinv, pattern)
    schur = own - jnp.dot(coupling, z_all, preferred_element_type=jnp.float32)
    left_cols = schur[:, :FACE]
    right_cols = schur[:, FACE:]
    new_a = assemble_a(left_cols[:FACE], orders[0])
    new_b = assemble_b(right_cols[FACE:], orders[1])
    top = jnp.concatenate([new_a, right_cols[:FACE]], axis=1)
    bottom = jnp.concatenate([left_cols[FACE:], new_b], axis=1)
    assembled = jnp.concatenate([top, bottom], axis=0)
    moved = lax.all_to_all(
        place_rows(assembled, target), "sy", split_axis=0, concat_axis=0, tiled=True
    )
    return moved[None, None]


def solution(mesh):
    return jax.shard_map(
        local,
        mesh=mesh,
        in_specs=(
            P("sx", "sy", None, None),
            P("sx", "sy", None, None),
            P("sx", "sy", None, None),
            P("sx", "sy", None, None, None, None),
            P("sx", "sy", None, None, None),
            P("sx", "sy", None, None),
            P("sx", "sy", None, None),
            P("sx", "sy", None),
        ),
        out_specs=P("sx", "sy", None, None),
        check_vma=False,
    )
```

profile of v0, /device:TPU:0, one launch (start us, length us, event | category | flops | bytes accessed | tf_op | source)
XLA Modules:
  0.0 255.2 jit_solution(18155242073711659802)
XLA Ops:
  0.0 0.0 copy-start
  0.0 3.7 %convolution_convert_fusion.3 = bf16[16,128,1024]{2,1,0:T(8,128)(2,1)S(1)} fusion(bf16[16,128,1024]{2,1,0:T(8,128)(2,1)} %bitcast.104, bf16[1,1,16,128,128]{4,3,2,1,0:T(8,128)(2,1)} %param.12), kind=kOutput, calls=%fused_computation.31 | convolution fusion | flops 538968064 | bytes 8912896 | tf_op jit(solution)/shard_map/bij,bjc->bic/dot_general | solution.py:35
  3.7 0.0 copy-start.3
  3.8 4.3 %copy.24 = bf16[2,8,128,1024]{3,1,2,0:T(8,128)(2,1)} copy(bf16[2,8,128,1024]{3,2,1,0:T(8,128)(2,1)S(1)} %bitcast.109) | data formatting | bytes 8388608
  8.1 0.0 copy-done.3
  8.1 0.1 copy.14
  8.2 0.1 eq.37
  8.3 10.5 %convolution_convert_fusion.2 = bf16[64,131072]{1,0:T(8,128)(2,1)} fusion(bf16[16,131072]{1,0:T(8,128)(2,1)} %bitcast.110, s32[64]{0:T(128)S(1)} %eq.37), kind=kOutput, calls=%fused_computation.2 | convolution fusion | flops 276825088 | bytes 20971776 | tf_op jit(solution)/shard_map/dot_general | solution.py:39
  18.8 0.0 copy-start.1
  18.8 18.7 %copy.25 = bf16[8,8,128,1024]{3,2,1,0:T(8,128)(2,1)} copy(bf16[8,8,128,1024]{3,1,2,0:T(8,128)(2,1)} %bitcast.99) | data formatting | bytes 33554432
  37.4 0.0 copy-done
  37.4 0.0 copy-done.1
  37.5 10.5 %convert_bitcast_fusion.1 = bf16[16,128,1024]{1,2,0:T(8,128)(2,1)} fusion(bf16[16,128,1024]{2,1,0:T(8,128)(2,1)} %bitcast.105, bf16[16,4,128,1024]{3,2,1,0:T(8,128)(2,1)} %bitcast.100, bf16[1,1,16,4,128,128]{5,4,3,2,1,0:T(8,128)(2,1)S(1)} %copy-done, bf16[1,1,16,128,128]{4,3,2,1,0:T(8,128)(2,1)S(1)} %copy-done.1), kind=kOutput, calls=%fused_computation.27 | convolution fusion | flops 2692743168 | bytes 27787264 | tf_op jit(solution)/shard_map/bij,bjc->bic/dot_general | solution.py:43
  47.9 6.8 %copy.26 = bf16[2,8,128,1024]{3,1,2,0:T(8,128)(2,1)} copy(bf16[2,8,128,1024]{2,3,1,0:T(8,128)(2,1)} %bitcast.112) | data formatting | bytes 8388608
  54.8 10.3 %convolution_convert_fusion.1 = bf16[64,131072]{1,0:T(8,128)(2,1)} fusion(bf16[16,131072]{1,0:T(8,128)(2,1)} %bitcast.113, s32[64]{0:T(128)S(1)} %eq.37), kind=kOutput, calls=%fused_computation.1 | convolution fusion | flops 276825088 | bytes 20971776 | tf_op jit(solution)/shard_map/dot_general | solution.py:39
  65.1 18.6 %copy.27 = bf16[8,8,128,1024]{3,2,1,0:T(8,128)(2,1)} copy(bf16[8,8,128,1024]{3,1,2,0:T(8,128)(2,1)} %bitcast.101) | data formatting | bytes 33554432
  83.7 10.7 %convert_bitcast_fusion = bf16[16,128,1024]{1,2,0:T(8,128)(2,1)} fusion(bf16[16,128,1024]{2,1,0:T(8,128)(2,1)} %bitcast.106, bf16[16,4,128,1024]{3,2,1,0:T(8,128)(2,1)} %bitcast.102, bf16[1,1,16,4,128,128]{5,4,3,2,1,0:T(8,128)(2,1)S(1)} %copy-done, bf16[1,1,16,128,128]{4,3,2,1,0:T(8,128)(2,1)S(1)} %copy-done.1), kind=kOutput, calls=%fused_computation.26 | convolution fusion | flops 2692743168 | bytes 27787264 | tf_op jit(solution)/shard_map/bij,bjc->bic/dot_general | solution.py:43
  94.3 6.8 %copy.28 = bf16[2,8,128,1024]{3,1,2,0:T(8,128)(2,1)} copy(bf16[2,8,128,1024]{2,3,1,0:T(8,128)(2,1)} %bitcast.114) | data formatting | bytes 8388608
  101.2 10.3 %convolution_convert_fusion = bf16[64,131072]{1,0:T(8,128)(2,1)} fusion(bf16[16,131072]{1,0:T(8,128)(2,1)} %bitcast.111, s32[64]{0:T(128)S(1)} %eq.37), kind=kOutput, calls=%fused_computation | convolution fusion | flops 276825088 | bytes 20971776 | tf_op jit(solution)/shard_map/dot_general | solution.py:39
  111.5 18.6 %copy.29 = bf16[8,8,128,1024]{3,2,1,0:T(8,128)(2,1)} copy(bf16[8,8,128,1024]{3,1,2,0:T(8,128)(2,1)} %bitcast.98) | data formatting | bytes 33554432
  130.1 10.5 %fusion.30 = bf16[16,1024,128]{1,2,0:T(8,128)(2,1)} fusion(bf16[16,128,1024]{2,1,0:T(8,128)(2,1)} %bitcast.107, bf16[16,4,128,1024]{3,2,1,0:T(8,128)(2,1)} %bitcast.103, bf16[1,1,16,4,128,128]{5,4,3,2,1,0:T(8,128)(2,1)S(1)} %copy-done, bf16[1,1,16,128,128]{4,3,2,1,0:T(8,128)(2,1)S(1)} %copy-done.1), kind=kOutput, calls=%fused_computation.30 | convolution fusion | flops 2692743168 | bytes 27787264 | tf_op jit(solution)/shard_map/bij,bjc->bic/dot_general | solution.py:43
  140.6 0.0 copy-start.2
  140.6 5.7 %copy.13 = f32[1,1,1024,1024]{2,3,1,0:T(8,128)} copy(f32[1,1,1024,1024]{3,2,1,0:T(8,128)} %param.10) | data formatting | bytes 8388608 | tf_op args[2]
  146.3 0.0 copy-done.2
  146.3 9.2 %bitcast_subtract_fusion = f32[1024,1024]{0,1:T(8,128)S(1)} fusion(f32[1,1,1024,1024]{2,3,1,0:T(8,128)} %copy.13, bf16[2048,1024]{1,0:T(8,128)(2,1)} %bitcast.116, bf16[1,1,1024,2048]{3,2,1,0:T(8,128)(2,1)} %param.9), kind=kOutput, calls=%fused_computation.23 | convolution fusion | flops 4296015872 | bytes 16777216 | tf_op jit(solution)/shard_map/dot_general | solution.py:99
  155.5 1.1 fusion.48
  156.7 1.2 fusion.47
  157.9 4.1 %collective-permute-start = (f32[512,512]{1,0:T(8,128)S(1)}, f32[512,512]{1,0:T(8,128)S(1)}, u32[]{:S(2)}, u32[]{:S(2)}) collective-permute-start(f32[512,512]{1,0:T(8,128)S(1)} %fusion.47), channel_id=1, source_target_pairs={{0,16},{16,0},{32,48},{48,32},{64,80},{80,64},{96,112},{112,96},{1... | collective-permute-start | bytes 3145736 | tf_op jit(solution)/shard_map/ppermute | solution.py:25
  161.9 1.1 fusion.45
  163.1 1.2 fusion.44
  164.2 0.3 collective-permute-start.1
  164.5 0.2 fusion.67
  164.7 20.4 %collective-permute-done = f32[512,512]{1,0:T(8,128)S(1)} collective-permute-done((f32[512,512]{1,0:T(8,128)S(1)}, f32[512,512]{1,0:T(8,128)S(1)}, u32[]{:S(2)}, u32[]{:S(2)}) %collective-permute-start) | collective-permute-done | bytes 1048608 | tf_op jit(solution)/shard_map/ppermute | solution.py:25
  185.1 1.2 fusion.46
  186.3 0.0 copy-start.4
  186.3 1.1 convolution_add_fusion.1
  187.4 0.0 collective-permute-done.1
  187.4 1.2 fusion.43
  188.6 1.1 convolution_add_fusion
  189.7 0.0 copy-done.4
  189.7 8.0 %fusion.15 = f32[1024,1024]{1,0:T(8,128)S(1)} fusion(f32[512,512]{0,1:T(8,128)S(1)} %convolution_add_fusion, f32[512,512]{0,1:T(8,128)S(1)} %get-tuple-element.6, f32[512,512]{0,1:T(8,128)S(1)} %get-tuple-element.5, f32[512,512]{0,1:T(8,128)S(1)} %convolution_add_fusion.1, s32[1024]{0:T(1024)S(1)} %bitcast.125), kind=kOutput, calls=%fused_computation.15 | convolution fusion | flops 12890144768 | bytes 8392704 | tf_op jit(solution)/shard_map/dot_general | solution.py:77
  197.8 55.3 %all_to_all.9 = f32[16,64,1024]{2,1,0:T(8,128)S(1)} all-to-all(f32[16,64,1024]{2,1,0:T(8,128)S(1)} %bitcast.115), channel_id=1, replica_groups=mesh['sx'=8,'sy'=16] {'sy'}, dimensions={0} | all-to-all | bytes 8388608 | tf_op jit(solution)/shard_map/all_to_all | solution.py:107
  253.0 2.0 copy.33
  (1 shorter events, 0.0 us)
Async XLA Ops:
  0.0 37.4 %copy-start = (bf16[1,1,16,4,128,128]{5,4,3,2,1,0:T(8,128)(2,1)S(1)}, bf16[1,1,16,4,128,128]{5,4,3,2,1,0:T(8,128)(2,1)}, u32[]{:S(2)}) copy-start(bf16[1,1,16,4,128,128]{5,4,3,2,1,0:T(8,128)(2,1)} %param.11) | copy-start | bytes 6291460
  3.7 4.4 %copy-start.3 = (s32[1,1,16,4]{2,3,1,0:T(4,128)S(1)}, s32[1,1,16,4]{2,3,1,0:T(4,128)}, u32[]{:S(2)}) copy-start(s32[1,1,16,4]{2,3,1,0:T(4,128)} %param.13) | copy-start | bytes 772
  18.8 18.7 %copy-start.1 = (bf16[1,1,16,128,128]{4,3,2,1,0:T(8,128)(2,1)S(1)}, bf16[1,1,16,128,128]{4,3,2,1,0:T(8,128)(2,1)}, u32[]{:S(2)}) copy-start(bf16[1,1,16,128,128]{4,3,2,1,0:T(8,128)(2,1)} %param.12) | copy-start | bytes 1572868
  140.6 5.7 %copy-start.2 = (s32[1,1,2,512]{3,2,1,0:T(2,128)S(1)}, s32[1,1,2,512]{3,2,1,0:T(2,128)}, u32[]{:S(2)}) copy-start(s32[1,1,2,512]{3,2,1,0:T(2,128)} %param.14) | copy-start | bytes 12292
  157.9 27.2 %collective-permute-start = (f32[512,512]{1,0:T(8,128)S(1)}, f32[512,512]{1,0:T(8,128)S(1)}, u32[]{:S(2)}, u32[]{:S(2)}) collective-permute-start(f32[512,512]{1,0:T(8,128)S(1)} %fusion.47), channel_id=1, source_target_pairs={{0,16},{16,0},{32,48},{48,32},{64,80},{80,64},{96,112},{112,96},{1... | collective-permute-start | bytes 3145736 | tf_op jit(solution)/shard_map/ppermute | solution.py:25
  164.2 23.2 %collective-permute-start.1 = (f32[512,512]{1,0:T(8,128)S(1)}, f32[512,512]{1,0:T(8,128)S(1)}, u32[]{:S(2)}, u32[]{:S(2)}) collective-permute-start(f32[512,512]{1,0:T(8,128)S(1)} %fusion.44), channel_id=1, source_target_pairs={{0,1},{1,0},{2,3},{3,2},{4,5},{5,4},{6,7},{7,6},{8,9},{9,8},{10,11... | collective-permute-start | bytes 3145736 | tf_op jit(solution)/shard_map/ppermute | solution.py:25
  186.3 3.5 %copy-start.4 = (s32[1,1,1024]{2,1,0:T(1,128)S(1)}, s32[1,1,1024]{2,1,0:T(1,128)}, u32[]{:S(2)}) copy-start(s32[1,1,1024]{2,1,0:T(1,128)} %param.15) | copy-start | bytes 12292
where the time goes:
time: 260 us; the launch traced here: 255 us
  matrix products  92.8 us (36%)
  local copies, waits for them, and re-layouts  82.1 us (32%)
  blocking collectives  55.3 us (21%)
  waiting for transfers between devices  20.4 us (8%)
  starting transfers between devices  4.32 us (2%)
    unnamed x19, local copies, waits for them, and re-layouts  81.8 us
    all_to_all x1, blocking collectives, local(): lax.all_to_all(place_rows(assembled, target), 'sy', split_axis=0, concat_...  55.3 us
    dot_general x3, matrix products, eliminate(): jnp.einsum('bij,bjc->bic', dinv, resid, preferred_element_type=jnp.float32)  31.6 us
    dot_general x3, matrix products, eliminate(): jnp.dot(picker, z_now.reshape(NB, BS * width), preferred_element_type=jnp...  31.1 us
    ppermute x2, waiting for transfers between devices, swapped(): return lax.ppermute(block, axis, route)  20.4 us
    dot_general x1, matrix products, local(): schur = own - jnp.dot(coupling, z_all, preferred_element_type=jnp.float32)  9.2 us
    dot_general x1, matrix products, place_rows(): jnp.dot(placer, tile, precision=exact, preferred_element_type=jnp.float32)  8.04 us
  transfers between devices with their start and end apart: 2, of which 1 were waited for; matrix products, arithmetic and copies ran while one was open for 2% of the time, Pallas kernels for 0%

commit v1 on v0

v1 whole, which is shorter than its diff:
```python
import functools

import jax
import jax.numpy as jnp
from jax import lax
from jax.experimental import pallas as pl
from jax.experimental.pallas import tpu as pltpu
from jax.sharding import PartitionSpec as P


BS = 128
FACE = 512
NB = 16
NNZ = 4
SWEEPS = 3
ROWS = 1024
NI = 2048
SHARE = 64
OWNERS = ROWS // SHARE
UNROLL = 8
PIECES = 4

f32, bf16 = jnp.float32, jnp.bfloat16
HBM = pl.BlockSpec(memory_space=pltpu.HBM)
VMEM = pl.BlockSpec(memory_space=pltpu.VMEM)
SMEM = pl.BlockSpec(memory_space=pltpu.SMEM)


def swapped(block, axis, bit):
    count = lax.axis_size(axis)
    return lax.ppermute(block, axis, [(low, low ^ 1 << bit) for low in range(count)])


def dot(a, b, dims=((1,), (0,))):
    return lax.dot_general(a, b, (dims, ((), ())), preferred_element_type=f32)


def over_blocks(body, low=0, high=NB, unroll=UNROLL):
    def some(i, carry):
        for u in range(unroll):
            body(low + i * unroll + u)
        return carry

    lax.fori_loop(0, (high - low) // unroll, some, 0)


def rows_of(b):
    return pl.ds(pl.multiple_of(b * BS, BS), BS)


def one_hot_t(order, count):
    width = order.shape[1]
    at = lax.broadcasted_iota(jnp.int32, (count, width), 0)
    return jnp.where(at == order, 1.0, 0.0).astype(bf16)


def schur_kernel(
    face, pattern, order, rhs_hbm, coupling_hbm, own_hbm, offs_hbm, dinv_hbm,
    shared_out, schur_out,
    rhs, coupling, own, offs, dinv, z, resid, sems,
):
    cols = pl.ds(face * FACE, FACE)
    step = NI // PIECES
    blocks = NB // PIECES
    rhs_in = [
        pltpu.make_async_copy(rhs_hbm.at[pl.ds(i * step, step), cols], rhs.at[pl.ds(i * step, step), :], sems.at[i])
        for i in range(PIECES)
    ]
    offs_in = [
        pltpu.make_async_copy(offs_hbm.at[pl.ds(i * blocks, blocks)], offs.at[pl.ds(i * blocks, blocks)], sems.at[PIECES + i])
        for i in range(PIECES)
    ]
    dinv_in = pltpu.make_async_copy(dinv_hbm, dinv, sems.at[2 * PIECES])
    own_in = pltpu.make_async_copy(own_hbm.at[:, cols], own, sems.at[2 * PIECES + 1])
    coupling_in = pltpu.make_async_copy(coupling_hbm, coupling, sems.at[2 * PIECES + 2])
    dinv_in.start()
    for copy in rhs_in + offs_in:
        copy.start()
    coupling_in.start()
    own_in.start()

    def first(b):
        z[rows_of(b), :] = dot(dinv[b], rhs[rows_of(b), :]).astype(bf16)

    dinv_in.wait()
    for i in range(PIECES):
        rhs_in[i].wait()
        over_blocks(first, i * blocks, (i + 1) * blocks, blocks)

    def residual(b):
        row = jnp.concatenate([offs[b, k] for k in range(NNZ)], axis=1)
        near = jnp.concatenate([z[rows_of(pattern[b, k]), :] for k in range(NNZ)], axis=0)
        resid[rows_of(b), :] = (rhs[rows_of(b), :].astype(f32) - dot(row, near)).astype(bf16)

    def relax(b):
        z[rows_of(b), :] = dot(dinv[b], resid[rows_of(b), :]).astype(bf16)

    for copy in offs_in:
        copy.wait()
    for _ in range(SWEEPS):
        over_blocks(residual)
        over_blocks(relax)

    coupling_in.wait()
    own_in.wait()
    for half in (face, 1 - face):
        rows = pl.ds(half * FACE, FACE)
        schur = (own[rows, :] - dot(coupling[rows, :], z[...])).astype(bf16)
        schur_out[rows, :] = schur
        if half == face:
            picker_t = one_hot_t(order[pl.ds(face, 1), :], FACE)
            right = dot(schur, picker_t).astype(bf16)
            shared_out[...] = dot(picker_t, right, ((0,), (0,)))


def schur_half(face, pattern, order, rhs, coupling, own, offs, dinv):
    return pl.pallas_call(
        functools.partial(schur_kernel, face),
        out_shape=(
            jax.ShapeDtypeStruct((FACE, FACE), f32),
            jax.ShapeDtypeStruct((ROWS, FACE), bf16),
        ),
        in_specs=[SMEM, VMEM, HBM, HBM, HBM, HBM, HBM],
        out_specs=(VMEM, VMEM),
        scratch_shapes=[
            pltpu.VMEM((NI, FACE), bf16),
            pltpu.VMEM((ROWS, NI), bf16),
            pltpu.VMEM((ROWS, FACE), f32),
            pltpu.VMEM((NB, NNZ, BS, BS), bf16),
            pltpu.VMEM((NB, BS, BS), bf16),
            pltpu.VMEM((NI, FACE), bf16),
            pltpu.VMEM((NI, FACE), bf16),
            pltpu.SemaphoreType.DMA((2 * PIECES + 3,)),
        ],
        cost_estimate=pl.CostEstimate(flops=9 * 10**9, bytes_accessed=12 * 2**20, transcendentals=0),
        compiler_params=pltpu.CompilerParams(vmem_limit_bytes=32 << 20),
    )(pattern, order, rhs, coupling, own, offs, dinv)


def place_kernel(order, target, left, right, left_out, right_out, left_to, right_to):
    placer = one_hot_t(target[...], ROWS)
    left_out[...] = dot(placer, left[...])
    right_out[...] = dot(placer, right[...])
    for face, out in ((0, left_to), (1, right_to)):
        picker_t = one_hot_t(order[pl.ds(face, 1), :], FACE)
        out[...] = dot(placer[:, face * FACE : (face + 1) * FACE], picker_t).astype(bf16)


def place(order, target, left, right):
    return pl.pallas_call(
        place_kernel,
        name="place",
        out_shape=(
            jax.ShapeDtypeStruct((ROWS, FACE), f32),
            jax.ShapeDtypeStruct((ROWS, FACE), f32),
            jax.ShapeDtypeStruct((ROWS, FACE), bf16),
            jax.ShapeDtypeStruct((ROWS, FACE), bf16),
        ),
        in_specs=[VMEM] * 4,
        out_specs=(VMEM,) * 4,
        cost_estimate=pl.CostEstimate(flops=4 * 10**9, bytes_accessed=8 * 2**20, transcendentals=0),
        compiler_params=pltpu.CompilerParams(vmem_limit_bytes=32 << 20),
    )(order, target, left, right)


def add_kernel(face, order, got, to, own, out_hbm, out, sems):
    picker_t = one_hot_t(order[pl.ds(face, 1), :], FACE)
    local = dot(got[...].astype(bf16), picker_t, ((1,), (1,))).astype(bf16)
    step = ROWS // PIECES
    copies = []
    for i in range(PIECES):
        rows = pl.ds(i * step, step)
        out[rows, :] = own[rows, :] + dot(to[rows, :], local)
        copies.append(pltpu.make_async_copy(out.at[rows, :], out_hbm.at[rows, :], sems.at[i]))
        copies[-1].start()
    for copy in copies:
        copy.wait()


def add_partner(face, order, got, to, own):
    return pl.pallas_call(
        functools.partial(add_kernel, face),
        out_shape=pltpu.HBM((ROWS, FACE), f32),
        in_specs=[VMEM] * 4,
        out_specs=HBM,
        scratch_shapes=[pltpu.VMEM((ROWS, FACE), f32), pltpu.SemaphoreType.DMA((PIECES,))],
        cost_estimate=pl.CostEstimate(flops=10**9, bytes_accessed=6 * 2**20, transcendentals=0),
        compiler_params=pltpu.CompilerParams(vmem_limit_bytes=24 << 20),
    )(order, got, to, own)


def to_owners(placed):
    return lax.all_to_all(placed.reshape(OWNERS, SHARE, FACE), "sy", split_axis=0, concat_axis=0, tiled=True)


def local(
    interior_rhs,
    interface_coupling,
    interface_local,
    off_blocks,
    diag_inverse,
    block_pattern,
    face_order,
    krylov_map,
):
    rhs, coupling, own, offs, dinv = (
        pltpu.with_memory_space_constraint(a[0, 0], pltpu.HBM)
        for a in (interior_rhs, interface_coupling, interface_local, off_blocks, diag_inverse)
    )
    pattern = block_pattern[0, 0]
    order = face_order[0, 0]
    target = krylov_map[0]
    half = functools.partial(
        schur_half, order=order, rhs=rhs, coupling=coupling, own=own, offs=offs, dinv=dinv
    )
    shared_a, left = half(0, pattern)
    got_a = swapped(shared_a, "sx", 0)
    left, pattern = lax.optimization_barrier((left, pattern))
    shared_b, right = half(1, pattern)
    got_b = swapped(shared_b, "sy", 0)
    left_own, right_own, left_to, right_to = place(order, target, left, right)
    right_sum = add_partner(1, order, got_b, right_to, right_own)
    right_all = to_owners(right_sum)
    got_a, right_sum = lax.optimization_barrier((got_a, right_sum))
    left_sum = add_partner(0, order, got_a, left_to, left_own)
    left_all = to_owners(left_sum)
    return jnp.concatenate([left_all, right_all], axis=2).reshape(1, 1, ROWS, ROWS)


def solution(mesh):
    return jax.shard_map(
        local,
        mesh=mesh,
        in_specs=(
            P("sx", "sy", None, None),
            P("sx", "sy", None, None),
            P("sx", "sy", None, None),
            P("sx", "sy", None, None, None, None),
            P("sx", "sy", None, None, None),
            P("sx", "sy", None, None),
            P("sx", "sy", None, None),
            P("sx", "sy", None),
        ),
        out_specs=P("sx", "sy", None, None),
        check_vma=False,
    )
```

time: 260 us -> 124 us (0.48); the launches traced: 255 us -> 123 us
  matrix products: 92.8 us -> 0 us
  local copies, waits for them, and re-layouts: 82.1 us -> 1.54 us
  Pallas kernels: 0 us -> 33.4 us
  blocking collectives: 55.3 us -> 63.4 us
    dot_general x17 -> x0, matrix products: 92.8 us -> none  [the longest x3 31.6 us: eliminate(): jnp.einsum('bij,bjc->bic', dinv, resid, preferred_element_type=jnp.float32)]
    unnamed x19 -> x10, local copies, waits for them, and re-layouts: 81.8 us -> 0.7 us
    pallas_call x0 -> x5, Pallas kernels: none -> 33.4 us  [the longest x2 25.9 us: schur_half(): pl.pallas_call(functools.partial(schur_kernel, face), out_shape=(jax.Shap...]
    all_to_all x1 -> x2, blocking collectives: 55.3 us -> 63.4 us  [to_owners(): lax.all_to_all(placed.reshape(OWNERS, SHARE, FACE), 'sy', split_axis=0, c...]
  transfers between devices with their start and end apart: 2 -> 2, of which waited for: 1 -> 1; matrix products, arithmetic and copies ran while one was open for 2% -> 0% of each run, Pallas kernels for 0% -> 4%
where the time goes in v1:
time: 124 us; the launch traced here: 123 us
  blocking collectives  63.4 us (51%)
  Pallas kernels  33.4 us (27%)
  waiting for transfers between devices  18.1 us (15%)
  starting transfers between devices  4.33 us (3%)
  other arithmetic  2.43 us (2%)
  local copies, waits for them, and re-layouts  1.54 us (1%)
    all_to_all x2, blocking collectives, to_owners(): lax.all_to_all(placed.reshape(OWNERS, SHARE, FACE), 'sy', split_axis=0, c...  63.4 us
    pallas_call x2, Pallas kernels, schur_half(): pl.pallas_call(functools.partial(schur_kernel, face), out_shape=(jax.Shap...  25.9 us
    ppermute x2, waiting for transfers between devices, swapped(): lax.ppermute(block, axis, [(low, low ^ 1 << bit) for low in range(count)])  18.1 us
    ppermute x2, starting transfers between devices, swapped(): lax.ppermute(block, axis, [(low, low ^ 1 << bit) for low in range(count)])  4.33 us
    pallas_call x2, Pallas kernels, add_partner(): pl.pallas_call(functools.partial(add_kernel, face), out_shape=pltpu.HBM((...  4.11 us
    pallas_call x1, Pallas kernels, place(): pl.pallas_call(place_kernel, name='place', out_shape=(jax.ShapeDtypeStruc...  3.42 us
  transfers between devices with their start and end apart: 2, of which 1 were waited for; matrix products, arithmetic and copies ran while one was open for 0% of the time, Pallas kernels for 4%

profile of v1, /device:TPU:0, one launch (start us, length us, event | category | flops | bytes accessed | tf_op | source)
XLA Modules:
  0.0 123.3 jit_solution(105433717450517382)
XLA Ops:
  0.0 0.8 copy.9.pattern
  0.8 0.0 copy-start
  0.8 0.7 copy-done
  1.4 0.0 copy-start.4
  1.4 0.0 copy-start.1
  1.4 13.0 %shard_map.82 = (f32[512,512]{1,0:T(8,128)S(1)}, bf16[1024,512]{1,0:T(8,128)(2,1)S(1)}) custom-call(s32[16,4]{1,0:T(8,128)S(1)} %copy.9.pattern, s32[2,512]{1,0:T(2,128)S(1)} %bitcast.11, bf16[2048,1024]{1,0:T(8,128)(2,1)} %bitcast.21, bf16[1024,2048]{1,0:T(8,128)(2,1)} %bitcast.23, f32[1024,1024]{1,0:T(8,128)} %bitcast.25, ...), custom_call_target="tpu_custom_call" | custom-call | flops 8999999488 | bytes 12582912 | tf_op jit(solution)/shard_map/pallas_call | solution.py:117
  14.4 0.0 copy-done.4
  14.4 0.1 copy.10.pattern
  14.5 0.0 copy-done.1
  14.5 0.0 copy-start.2
  14.5 12.9 %shard_map.83 = (f32[512,512]{1,0:T(8,128)S(1)}, bf16[1024,512]{1,0:T(8,128)(2,1)S(1)}) custom-call(s32[16,4]{1,0:T(8,128)S(1)} %copy.10.pattern, s32[2,512]{1,0:T(2,128)S(1)} %bitcast.12, bf16[2048,1024]{1,0:T(8,128)(2,1)} %bitcast.22, bf16[1024,2048]{1,0:T(8,128)(2,1)} %bitcast.24, f32[1024,1024]{1,0:T(8,128)} %bitcast.26, ...), custom_call_target="tpu_custom_call" | custom-call | flops 8999999488 | bytes 12582912 | tf_op jit(solution)/shard_map/pallas_call | solution.py:117
  27.5 0.1 collective-permute-start.1
  27.5 4.2 %collective-permute-start = (f32[512,512]{1,0:T(8,128)S(1)}, f32[512,512]{1,0:T(8,128)S(1)}, u32[]{:S(2)}, u32[]{:S(2)}) collective-permute-start(f32[512,512]{1,0:T(8,128)S(1)} %get-tuple-element.16), channel_id=1, source_target_pairs={{0,16},{16,0},{32,48},{48,32},{64,80},{80,64},{96,112},{112,96},{1... | collective-permute-start | bytes 3145736 | tf_op jit(solution)/shard_map/ppermute | solution.py:31
  31.8 0.0 copy-done.2
  31.8 3.4 %place.1 = (f32[1024,512]{1,0:T(8,128)S(1)}, f32[1024,512]{1,0:T(8,128)S(1)}, bf16[1024,512]{1,0:T(8,128)(2,1)S(1)}, bf16[1024,512]{1,0:T(8,128)(2,1)S(1)}) custom-call(s32[2,512]{1,0:T(2,128)S(1)} %bitcast.13, s32[1,1024]{1,0:T(1,128)S(1)} %bitcast.16, bf16[1024,512]{1,0:T(8,128)(2,1)S(1)} %get-tuple-element.20.left, ...), custom_call_target="tpu_custom_call" | custom-call | flops 4000000000 | bytes 8388608 | tf_op jit(solution)/shard_map/place/pallas_call | solution.py:150
  35.2 0.0 collective-permute-done.1.got
  35.2 2.0 %shard_map.84 = f32[1024,512]{1,0:T(8,128)} custom-call(s32[2,512]{1,0:T(2,128)S(1)} %bitcast.14, f32[512,512]{1,0:T(8,128)S(1)} %collective-permute-done.1.got, bf16[1024,512]{1,0:T(8,128)(2,1)S(1)} %get-tuple-element.22.to, f32[1024,512]{1,0:T(8,128)S(1)} %get-tuple-element.23.own), custom_call_target="tpu_custom_call" | custom-call | flops 1000000000 | bytes 6291456 | tf_op jit(solution)/shard_map/pallas_call | solution.py:181
  37.3 18.1 %collective-permute-done.got = f32[512,512]{1,0:T(8,128)S(1)} collective-permute-done((f32[512,512]{1,0:T(8,128)S(1)}, f32[512,512]{1,0:T(8,128)S(1)}, u32[]{:S(2)}, u32[]{:S(2)}) %collective-permute-start) | collective-permute-done | bytes 1048608 | tf_op jit(solution)/shard_map/ppermute | solution.py:31
  55.4 2.1 %shard_map.85 = f32[1024,512]{1,0:T(8,128)} custom-call(s32[2,512]{1,0:T(2,128)S(1)} %bitcast.15, f32[512,512]{1,0:T(8,128)S(1)} %collective-permute-done.got, bf16[1024,512]{1,0:T(8,128)(2,1)S(1)} %get-tuple-element.25.to, f32[1024,512]{1,0:T(8,128)S(1)} %get-tuple-element.26.own), custom_call_target="tpu_custom_call" | custom-call | flops 1000000000 | bytes 6291456 | tf_op jit(solution)/shard_map/pallas_call | solution.py:181
  57.4 0.0 copy-start.3
  57.4 33.1 %all_to_all.10 = f32[16,64,512]{2,1,0:T(8,128)S(1)} all-to-all(f32[16,64,512]{2,1,0:T(8,128)} %bitcast.18), channel_id=1, replica_groups=mesh['sx'=8,'sy'=16] {'sy'}, dimensions={0} | all-to-all | bytes 4194304 | tf_op jit(solution)/shard_map/all_to_all | solution.py:193
  90.6 0.0 copy-done.3
  90.6 30.3 %all_to_all.11 = f32[16,64,512]{2,1,0:T(8,128)S(1)} all-to-all(f32[16,64,512]{2,1,0:T(8,128)S(1)} %bitcast.17), channel_id=1, replica_groups=mesh['sx'=8,'sy'=16] {'sy'}, dimensions={0} | all-to-all | bytes 4194304 | tf_op jit(solution)/shard_map/all_to_all | solution.py:193
  120.9 2.4 %pad_maximum_fusion = f32[16,64,1024]{2,1,0:T(8,128)} fusion(f32[16,64,512]{2,1,0:T(8,128)S(1)} %all_to_all.11, f32[16,64,512]{2,1,0:T(8,128)S(1)} %all_to_all.10), kind=kLoop, calls=%fused_computation | loop fusion | flops 1048576 | bytes 8388608 | tf_op jit(solution)/shard_map/concatenate | solution.py:227
Async XLA Ops:
  0.8 0.7 copy-start
  1.4 13.0 %copy-start.4 = (s32[1,1,16,4]{2,3,1,0:T(4,128)S(1)}, s32[1,1,16,4]{2,3,1,0:T(4,128)}, u32[]{:S(2)}) copy-start(s32[1,1,16,4]{2,3,1,0:T(4,128)} %param.13) | copy-start | bytes 772
  1.4 13.1 %copy-start.1 = (s32[1,1,2,512]{3,2,1,0:T(2,128)S(1)}, s32[1,1,2,512]{3,2,1,0:T(2,128)}, u32[]{:S(2)}) copy-start(s32[1,1,2,512]{3,2,1,0:T(2,128)} %param.14) | copy-start | bytes 12292
  14.5 17.3 %copy-start.2 = (s32[1,1,1024]{2,1,0:T(1,128)S(1)}, s32[1,1,1024]{2,1,0:T(1,128)}, u32[]{:S(2)}) copy-start(s32[1,1,1024]{2,1,0:T(1,128)} %param.15) | copy-start | bytes 12292
  27.5 7.8 %collective-permute-start.1 = (f32[512,512]{1,0:T(8,128)S(1)}, f32[512,512]{1,0:T(8,128)S(1)}, u32[]{:S(2)}, u32[]{:S(2)}) collective-permute-start(f32[512,512]{1,0:T(8,128)S(1)} %get-tuple-element.19), channel_id=1, source_target_pairs={{0,1},{1,0},{2,3},{3,2},{4,5},{5,4},{6,7},{7,6},{8,9},{9,8},{10,11... | collective-permute-start | bytes 3145736 | tf_op jit(solution)/shard_map/ppermute | solution.py:31
  27.5 27.8 %collective-permute-start = (f32[512,512]{1,0:T(8,128)S(1)}, f32[512,512]{1,0:T(8,128)S(1)}, u32[]{:S(2)}, u32[]{:S(2)}) collective-permute-start(f32[512,512]{1,0:T(8,128)S(1)} %get-tuple-element.16), channel_id=1, source_target_pairs={{0,16},{16,0},{32,48},{48,32},{64,80},{80,64},{96,112},{112,96},{1... | collective-permute-start | bytes 3145736 | tf_op jit(solution)/shard_map/ppermute | solution.py:31
  57.4 33.1 %copy-start.3 = (f32[1024,512]{1,0:T(8,128)S(1)}, f32[1024,512]{1,0:T(8,128)}, u32[]{:S(2)}) copy-start(f32[1024,512]{1,0:T(8,128)} %shard_map.84) | copy-start | bytes 6291460
